TPU v7x, 32 devices: a whole 2x2x4 slice. The times are simulated.
32 devices in a mesh: groups: 2 (over y), req: 2 (over x), head: 4 (over z), sec: 2 (over core).
Axes of the slice: x: 2, y: 2, z: 4, core: 2. Of those that a mesh axis runs over, the one named last changes fastest.
Arguments:
- queries: bfloat16 [512, 4096], P(('groups', 'req'), ('head', 'sec')), parts along dimension 0, may hold values from -16 to 16
- cache_pool: bfloat16 [48, 128, 8, 128], P(('groups', 'req'), None, 'head'), parts along dimension 0, may hold values from -4 to 4
- lengths: int32 [4], P(('groups', 'req')), parts along dimension 0, may hold values from 128 to 1536, as said below
- block_table: int32 [4, 12], P(('groups', 'req')), parts along dimension 0, may hold values from 0 to 11, as said below
- out_proj: bfloat16 [4096, 2880], P(('head', 'sec')), may hold values from -0.375 to 0.375
- residual_in: bfloat16 [512, 2880], P(('groups', 'req', 'head', 'sec')), parts along dimension 0, may hold values from -16 to 16
- norm_gain: float32 [2880], replicated, may hold values from 0.1 to 1.9
- expert_ids: int32 [512, 4], P(('groups', 'req', 'head', 'sec')), parts along dimension 0, may hold values from 0 to 7, all different within a row; in each aligned block of 16 rows (0 to 15, 16 to 31, ...) at most 8 rows name the same one
- route_weight: float32 [512, 4], P(('groups', 'req', 'head', 'sec')), parts along dimension 0, may hold values from 0.2 to 1
- gate_weight: bfloat16 [8, 2880, 2880], P(('head', 'sec'), None, 'req'), may hold values from -0.109375 to 0.109375
- up_weight: bfloat16 [8, 2880, 2880], P(('head', 'sec'), None, 'req'), may hold values from -0.109375 to 0.109375
- down_weight: bfloat16 [8, 2880, 2880], P(('head', 'sec'), 'req'), may hold values from -0.109375 to 0.109375
Outputs:
- layer_out: bfloat16 [512, 2880], P(('groups', 'req', 'head', 'sec')), parts along dimension 0
There are 2 independent parts, one for each index of `groups`. A program takes and returns all parts, laid end to end along the dimension named above; an argument that names none is the same for every part. Nothing has to cross between parts.
Inputs may be any that keep to these rules, and one draw needn't show every extreme that they name: lengths[r] counts request r's positions, its last 128 positions being its new rows; some request reaches 1536 in every draw. `block_table`: each row is a permutation of 0 to 11. `expert_ids`: a row names 4 different experts; in each aligned block of 16 rows every expert is named by exactly 8 rows.
All inputs are finite; a program needn't handle non-finite values.
Results may differ from a plain program's by a relative error of at most 0.017.
Values may be sent and summed in bfloat16 or wider, within the bound.
A program may use at most 128 MiB of HBM per device.

v0:
```python
import math
import jax
import jax.numpy as jnp
from jax import lax
from jax.sharding import PartitionSpec as P

QH = 64
KVH = 8
TOP = 4
EPSILON = 1e-05
MASKED = -1e30


def run_expert(row_block, gate_weight, up_weight, down_weight):
    row_shape = row_block.shape
    flat_rows = row_block.reshape(-1, row_shape[-1])
    gate_out = jnp.dot(flat_rows, gate_weight[0], preferred_element_type=jnp.float32)
    up_out = jnp.dot(flat_rows, up_weight[0], preferred_element_type=jnp.float32)
    activated = (gate_out * jax.nn.sigmoid(1.702 * gate_out) * (up_out + 1.0)).astype(jnp.bfloat16)
    partial_value = jnp.dot(activated, down_weight[0], preferred_element_type=jnp.float32)
    return partial_value.astype(jnp.bfloat16).reshape(row_shape[:-1] + (partial_value.shape[-1],))


def masked_scores(query_heads, key_block, positions, score_scale):
    scores = (
        jnp.einsum("nhd,thd->hnt", query_heads, key_block, preferred_element_type=jnp.float32)
        * score_scale
    )
    key_positions = jnp.arange(key_block.shape[0], dtype=jnp.int32)
    visible = key_positions[None, None, :] <= positions[None, :, None]
    return jnp.where(visible, scores, MASKED)


def on_device(
    queries,
    cache_pool,
    lengths,
    block_table,
    out_proj,
    residual_in,
    norm_gain,
    expert_ids,
    route_weight,
    gate_weight,
    up_weight,
    down_weight,
):
    head_dim = cache_pool.shape[3] // 2
    block_len = cache_pool.shape[1]
    max_blocks = cache_pool.shape[0]
    new_rows = queries.shape[0]
    local_heads = queries.shape[1] // head_dim
    score_scale = 1.0 / math.sqrt(head_dim)
    context = lengths[0]
    sequence = cache_pool[block_table[0]]
    kv_choice = (
        lax.axis_index("sec") * local_heads + jnp.arange(local_heads, dtype=jnp.int32)
    ) // (QH // KVH)
    selected = jnp.take(sequence, kv_choice, axis=2)
    key_heads = selected[..., :head_dim]
    value_heads = selected[..., head_dim:]
    query_heads = queries.reshape(new_rows, local_heads, head_dim)
    positions = context - new_rows + jnp.arange(new_rows, dtype=jnp.int32)
    all_keys = key_heads.reshape(max_blocks * block_len, local_heads, head_dim)
    all_values = value_heads.reshape(max_blocks * block_len, local_heads, head_dim)
    scores = masked_scores(query_heads, all_keys, positions, score_scale)
    row_max = jnp.max(scores, axis=-1, keepdims=True)
    exp_scores = jnp.exp(scores - row_max)
    row_sum = jnp.sum(exp_scores, axis=-1, keepdims=True)
    probabilities = (exp_scores / row_sum).astype(jnp.bfloat16)
    attended = jnp.einsum(
        "hnt,thd->nhd", probabilities, all_values, preferred_element_type=jnp.float32
    )
    attn = attended.astype(jnp.bfloat16).reshape(new_rows, local_heads * head_dim)
    share_rows = new_rows // (lax.axis_size("head") * lax.axis_size("sec"))
    partial_value = jnp.dot(attn, out_proj, preferred_element_type=jnp.float32)
    projected = lax.psum_scatter(
        partial_value.astype(jnp.bfloat16).astype(jnp.float32).astype(jnp.bfloat16),
        ("head", "sec"),
        scatter_dimension=0,
        tiled=True,
    ).astype(jnp.float32)
    residual = (residual_in.astype(jnp.float32) + projected).astype(jnp.bfloat16)
    residual_wide = residual.astype(jnp.float32)
    mean_square = jnp.mean(residual_wide * residual_wide, axis=-1, keepdims=True)
    normed = (residual_wide * lax.rsqrt(mean_square + EPSILON) * norm_gain).astype(jnp.bfloat16)
    experts_all = lax.axis_size("head") * lax.axis_size("sec")
    capacity = share_rows * TOP // experts_all
    flat_ids = expert_ids.reshape(-1)
    onehot = (flat_ids[:, None] == jnp.arange(experts_all, dtype=jnp.int32)[None, :]).astype(
        jnp.int32
    )
    before = jnp.cumsum(onehot, axis=0) - onehot
    target = flat_ids * capacity + jnp.sum(before * onehot, axis=1)
    source_row = (
        jnp.zeros((experts_all * capacity,), jnp.int32)
        .at[target]
        .set(jnp.arange(share_rows * TOP, dtype=jnp.int32) // TOP)
    )
    buffer = normed[source_row].reshape(experts_all, capacity, normed.shape[1])
    copies = lax.all_gather(buffer[None], "req", axis=0, tiled=True)
    results = run_expert(
        lax.all_to_all(copies, ("head", "sec"), split_axis=1, concat_axis=1, tiled=True),
        gate_weight,
        up_weight,
        down_weight,
    )
    partial_back = lax.all_to_all(results, ("head", "sec"), split_axis=1, concat_axis=1, tiled=True)
    returned = (
        lax.psum_scatter(
            partial_back.astype(jnp.float32).astype(jnp.bfloat16),
            "req",
            scatter_dimension=0,
            tiled=True,
        )
        .astype(jnp.float32)[0]
        .astype(jnp.bfloat16)
    )
    gathered_out = returned.reshape(experts_all * capacity, -1)[target].reshape(share_rows, TOP, -1)
    expert_mix = jnp.sum(route_weight[:, :, None] * gathered_out.astype(jnp.float32), axis=1)
    return (residual.astype(jnp.float32) + expert_mix).astype(jnp.bfloat16)


def solution(mesh):
    return jax.shard_map(
        on_device,
        mesh=mesh,
        in_specs=(
            P(("groups", "req"), ("head", "sec")),
            P(("groups", "req"), None, "head", None),
            P(("groups", "req")),
            P(("groups", "req"), None),
            P(("head", "sec"), None),
            P(("groups", "req", "head", "sec"), None),
            P(),
            P(("groups", "req", "head", "sec"), None),
            P(("groups", "req", "head", "sec"), None),
            P(("head", "sec"), None, "req"),
            P(("head", "sec"), None, "req"),
            P(("head", "sec"), "req", None),
        ),
        out_specs=P(("groups", "req", "head", "sec"), None),
        check_vma=False,
    )
```

profile of v0, /device:TPU:0, one launch (start us, length us, event | category | flops | bytes accessed | tf_op | source)
XLA Modules:
  0.0 203.9 jit_solution(17053103708731632131)
XLA Ops:
  7.4 4.3 %gather_fusion = bf16[12,128,2,128]{3,2,1,0:T(2,128)(2,1)} fusion(bf16[12,128,2,128]{3,2,1,0:T(2,128)(2,1)} %param.13, s32[1024]{0:T(1024)S(1)} %pad_clamp_fusion.3), kind=kCustom, calls=%fused_computation | custom fusion | bytes 1572912 | tf_op jit(solution)/shard_map/gather | solution.py:55
  11.7 2.2 %copy.61 = bf16[12,128,2,128]{3,1,2,0:T(8,128)(2,1)} copy(bf16[12,128,2,128]{3,2,1,0:T(2,128)(2,1)} %gather_fusion) | data formatting | bytes 1572864 | tf_op jit(solution)/shard_map/gather | solution.py:55
  13.9 3.7 %gather_fusion.1 = bf16[8,12,128,128]{3,2,1,0:T(8,128)(2,1)} fusion(bf16[12,128,2,128]{3,1,2,0:T(8,128)(2,1)} %copy.61, s32[1024]{0:T(1024)S(1)} %pad_clamp_fusion.2), kind=kCustom, calls=%fused_computation.1 | custom fusion | bytes 6291488 | tf_op jit(solution)/shard_map/jit(_take)/gather | solution.py:59
  17.6 2.3 %select_bitcast_fusion = bf16[12,128,8,128]{3,1,0,2:T(8,128)(2,1)S(1)} fusion(bf16[8,12,128,128]{3,2,1,0:T(8,128)(2,1)} %gather_fusion.1, pred[8]{0:T(512)(128)(4,1)S(1)} %compare_and_fusion), kind=kLoop, calls=%fused_computation.18 | loop fusion | flops 1572864 | bytes 6291464 | tf_op jit(solution)/shard_map/jit(_take)/select_n | solution.py:59
  19.9 3.8 %fusion.50 = (bf16[12,128,8,64]{3,1,0,2:T(8,128)(2,1)}, bf16[12,128,8,64]{3,1,0,2:T(8,128)(2,1)}) fusion(bf16[12,128,8,128]{3,1,0,2:T(8,128)(2,1)S(1)} %select_bitcast_fusion), kind=kLoop, calls=%fused_computation.82 | loop fusion | bytes 6291456 | tf_op jit(solution)/shard_map/slice | solution.py:60
  24.7 4.1 %fusion.51 = f32[8,128]{1,0:T(8,128)S(1)} fusion(pred[128,1536]{0,1:T(8,128)(4,1)S(1)} %iota_compare_fusion, bf16[1536,8,64]{2,0,1:T(8,128)(2,1)} %bitcast.70, bf16[128,8,64]{0,2,1:T(8,128)(2,1)S(1)} %bitcast.75), kind=kOutput, calls=%fused_computation.83 | convolution fusion | flops 207619584 | bytes 1904640 | tf_op jit(solution)/shard_map/sub | solution.py:68
  28.7 5.8 %fusion.24 = bf16[8,64,128]{2,1,0:T(8,128)(2,1)S(1)} fusion(bf16[1536,8,64]{2,0,1:T(8,128)(2,1)} %bitcast.72, f32[8,128]{1,0:T(8,128)S(1)} %fusion.51, pred[128,1536]{0,1:T(8,128)(4,1)S(1)} %iota_compare_fusion, bf16[1536,8,64]{2,0,1:T(8,128)(2,1)} %bitcast.71, bf16[128,8,64]{0,2,1:T(8,128)(2,1)S(1)} %bitcast.76), kind=kOutput, calls=%fused_computation.26 | convolution fusion | flops 410585600 | bytes 3608576 | tf_op jit(solution)/shard_map/hnt,thd->nhd/dot_general | solution.py:71
  34.6 2.0 convolution_convert_fusion
  38.2 32.8 %reduce-scatter.3.cloned.1.call-done = bf16[16,2880]{1,0:T(8,128)(2,1)} async-done(((bf16[128,2880]{1,0:T(8,128)(2,1)}), bf16[16,2880]{1,0:T(8,128)(2,1)}) %reduce-scatter.3.cloned.1.call-update) | async-done | bytes 92176 | tf_op jit(solution)/shard_map/reduce_scatter | solution.py:77
  71.0 1.0 fusion.31
  72.0 1.0 fusion.33
  73.8 8.3 %all_gather.3 = bf16[2,8,8,2880]{3,2,1,0:T(8,128)(2,1)S(1)} all-gather(bf16[1,8,8,2880]{3,2,1,0:T(8,128)(2,1)S(1)} %bitcast.74), channel_id=1, replica_groups=mesh['groups'=2,'req'=2,'head'=4,'sec'=2] {'req'}, dimensions={0}, use_global_device_ids=true | all-gather | bytes 1105920 | tf_op jit(solution)/shard_map/all_gather | solution.py:101
  82.2 24.9 %all_to_all.10 = bf16[2,8,8,2880]{3,2,0,1:T(8,128)(2,1)S(1)} all-to-all(bf16[2,8,8,2880]{3,2,0,1:T(8,128)(2,1)S(1)} %copy.69), channel_id=1, replica_groups=mesh['groups'=2,'req'=2,'head'=4,'sec'=2] {'head','sec'}, dimensions={1} | all-to-all | bytes 1474560 | tf_op jit(solution)/shard_map/all_to_all | solution.py:103
  107.1 0.9 copy-done.1
  108.0 6.7 %fusion.5 = f32[128,1440]{0,1:T(8,128)} fusion(bf16[128,2880]{1,0:T(8,128)(2,1)S(1)} %bitcast.68, bf16[1,2880,1440]{1,2,0:T(8,128)(2,1)} %param.21), kind=kOutput, calls=%fused_computation.10 | convolution fusion | flops 1061683200 | bytes 9768960 | tf_op jit(solution)/shard_map/dot_general | solution.py:17
  114.7 15.6 %fusion.8 = bf16[128,2880]{0,1:T(8,128)(2,1)} fusion(bf16[1,1440,2880]{2,1,0:T(8,128)(2,1)} %param.23, bf16[128,2880]{1,0:T(8,128)(2,1)} %bitcast.69, bf16[1,2880,1440]{1,2,0:T(8,128)(2,1)} %param.22, f32[128,1440]{0,1:T(8,128)} %fusion.5), kind=kOutput, calls=%fused_computation.16 | convolution fusion | flops 2125209600 | bytes 18800640 | tf_op jit(solution)/shard_map/dot_general | solution.py:20
  130.3 2.3 %copy.71 = bf16[128,2880]{1,0:T(8,128)(2,1)} copy(bf16[128,2880]{0,1:T(8,128)(2,1)} %fusion.8) | data formatting | bytes 1474560 | tf_op jit(solution)/shard_map/convert_element_type | solution.py:21
  132.6 1.2 copy.72
  133.8 23.4 %all_to_all.11 = bf16[2,8,8,2880]{3,2,0,1:T(8,128)(2,1)} all-to-all(bf16[2,8,8,2880]{3,2,0,1:T(8,128)(2,1)S(1)} %copy.72), channel_id=1, replica_groups=mesh['groups'=2,'req'=2,'head'=4,'sec'=2] {'head','sec'}, dimensions={1} | all-to-all | bytes 1474560 | tf_op jit(solution)/shard_map/all_to_all | solution.py:108
  157.9 31.6 %all-reduce.3.cloned.1.call-done = bf16[2,8,8,2880]{3,2,0,1:T(8,128)(2,1)} async-done(((bf16[2,8,8,2880]{3,2,0,1:T(8,128)(2,1)}), bf16[2,8,8,2880]{3,2,0,1:T(8,128)(2,1)}) %all-reduce.3.cloned.1.call-update) | async-done | bytes 737296
  189.5 1.7 dynamic-slice_bitcast_fusion
  191.2 1.5 gather_fusion.3
  192.7 2.0 %reshape.195 = f32[16,4,2880]{2,1,0:T(4,128)} reshape(bf16[64,2880]{1,0:T(8,128)(2,1)} %gather_fusion.3) | data formatting | bytes 1105920 | tf_op jit(solution)/shard_map/convert_element_type | solution.py:120
  194.7 1.7 multiply_reduce_fusion
  (50 shorter events, 5.0 us)
Async XLA Ops:
  6.5 28.1 %copy-start = (bf16[512,2880]{0,1:T(8,128)(2,1)S(1)}, bf16[512,2880]{0,1:T(8,128)(2,1)}, u32[]{:S(2)}) copy-start(bf16[512,2880]{0,1:T(8,128)(2,1)} %param.16) | copy-start | bytes 8847364
  6.5 64.5 %reduce-scatter.3.cloned.1.call-start = ((), (), s32[]{:S(2)}) async-start(), calls=%async_computation.3 | async-start | bytes 847872 | tf_op jit(solution)/shard_map/reduce_scatter | solution.py:77
  19.9 4.7 %copy-start.4 = (bf16[128,512]{1,0:T(8,128)(2,1)S(1)}, bf16[128,512]{1,0:T(8,128)(2,1)}, u32[]{:S(2)}) copy-start(bf16[128,512]{1,0:T(8,128)(2,1)} %param.12) | copy-start | bytes 393220
  34.6 2.1 %copy-start.6 = (s32[16,4]{0,1:T(4,128)S(1)}, s32[16,4]{0,1:T(4,128)}, u32[]{:S(2)}) copy-start(s32[16,4]{0,1:T(4,128)} %param.19) | copy-start | bytes 772
  34.6 36.4 %copy-start.2 = (bf16[16,2880]{1,0:T(8,128)(2,1)S(1)}, bf16[16,2880]{1,0:T(8,128)(2,1)}, u32[]{:S(2)}) copy-start(bf16[16,2880]{1,0:T(8,128)(2,1)} %param.17) | copy-start | bytes 276484
  34.6 37.5 %copy-start.5 = (f32[2880]{0:T(1024)S(1)}, f32[2880]{0:T(1024)}, u32[]{:S(2)}) copy-start(f32[2880]{0:T(1024)} %param.18) | copy-start | bytes 34564
  36.6 152.9 %all-reduce.3.cloned.1.call-start = ((), (), s32[]{:S(2)}) async-start(), calls=%async_computation.4 | async-start | bytes 1507328
  107.1 0.9 copy-start.1
  130.3 26.9 %copy-start.7 = (f32[16,4]{0,1:T(4,128)S(1)}, f32[16,4]{0,1:T(4,128)}, u32[]{:S(2)}) copy-start(f32[16,4]{0,1:T(4,128)} %param.20) | copy-start | bytes 772
  130.3 27.0 %copy-start.8 = (u32[32]{0:T(128)S(1)}, u32[32]{0:T(128)}, u32[]{:S(2)}) copy-start(u32[32]{0:T(128)} %constant.94) | copy-start | bytes 388
  157.2 39.2 %copy-start.3 = (bf16[16,2880]{1,0:T(8,128)(2,1)S(1)}, bf16[16,2880]{1,0:T(8,128)(2,1)}, u32[]{:S(2)}) copy-start(bf16[16,2880]{1,0:T(8,128)(2,1)} %reduce-scatter.3.cloned.1.call-done) | copy-start | bytes 276484
Sparse Core Ops, SparseCore 0:
  36.7 34.2 reduce-scatter.2
  157.3 32.1 all-reduce.2
where the time goes:
time: 205 us; the launch traced here: 204 us
  waiting for transfers between devices  64.4 us (31%)
  blocking collectives  56.5 us (28%)
  matrix products  34.2 us (17%)
  local copies, waits for them, and re-layouts  26.4 us (13%)
  between operations  14.3 us (7%)
  other arithmetic  7.99 us (4%)
    reduce_scatter x1, waiting for transfers between devices, on_device(): lax.psum_scatter(partial_value.astype(jnp.bfloat16).astype(jnp.float32).a...  32.8 us
    unnamed x3, waiting for transfers between devices  31.7 us
    all_to_all x1, blocking collectives, on_device(): lax.all_to_all(copies, ('head', 'sec'), split_axis=1, concat_axis=1, tile...  24.9 us
    all_to_all x1, blocking collectives, on_device(): lax.all_to_all(results, ('head', 'sec'), split_axis=1, concat_axis=1, til...  23.4 us
    dot_general x1, matrix products, run_expert(): jnp.dot(activated, down_weight[0], preferred_element_type=jnp.float32)  15.6 us
    all_gather x1, blocking collectives, on_device(): copies = lax.all_gather(buffer[None], 'req', axis=0, tiled=True)  8.28 us
    dot_general x1, matrix products, run_expert(): jnp.dot(flat_rows, gate_weight[0], preferred_element_type=jnp.float32)  6.69 us
    gather x2, local copies, waits for them, and re-layouts, on_device(): sequence = cache_pool[block_table[0]]  6.47 us
  transfers between devices with their start and end apart: 2, of which 2 were waited for; matrix products, arithmetic and copies ran while one was open for 1% of the time, Pallas kernels for 0%

commit v1 on v0

--- a/solution.py
+++ b/solution.py
@@ -105,7 +105,20 @@
         up_weight,
         down_weight,
     )
-    partial_back = lax.all_to_all(results, ("head", "sec"), split_axis=1, concat_axis=1, tiled=True)
+    ways, here = (lax.axis_size(("head", "sec")), lax.axis_index(("head", "sec")))
+    width = results.shape[1] // ways
+    lengths_2 = list(results.shape)
+    lengths_2[1] = width
+    height = lengths_2[1]
+    lengths_2[1] = height * ways
+    partial_back = jnp.zeros(lengths_2, results.dtype)
+    for mask in range(ways):
+        part = lax.dynamic_slice_in_dim(results, (here ^ mask) * width, width, axis=1)
+        if mask:
+            part = lax.ppermute(part, ("head", "sec"), [(d, d ^ mask) for d in range(ways)])
+        partial_back = lax.dynamic_update_slice_in_dim(
+            partial_back, part, (here ^ mask) * height, axis=1
+        )
     returned = (
         lax.psum_scatter(
             partial_back.astype(jnp.float32).astype(jnp.bfloat16),

time: 205 us -> 188 us (0.917)
  blocking collectives: 56.5 us -> 8.28 us
  starting transfers between devices: 0.04 us -> 13.1 us
  waiting for transfers between devices: 64.4 us -> 77.3 us
  local copies, waits for them, and re-layouts: 26.4 us -> 32.1 us
    all_to_all x2 -> x0, blocking collectives: 48.3 us -> none  [the longest x1 24.9 us: on_device(): lax.all_to_all(copies, ('head', 'sec'), split_axis=1, concat_axis=1, tile...]
    unnamed x3 -> x2, waiting for transfers between devices: 31.7 us -> 0.03 us
    all_to_all x0 -> x1, waiting for transfers between devices: none -> 20.1 us  [on_device(): lax.all_to_all(copies, ('head', 'sec'), split_axis=1, concat_axis=1, tile...]
    reduce_scatter x0 -> x1, waiting for transfers between devices: none -> 17.8 us  [on_device(): lax.psum_scatter(partial_back.astype(jnp.float32).astype(jnp.bfloat16), '...]
    ppermute x0 -> x7, starting transfers between devices: none -> 8.05 us  [on_device(): lax.ppermute(part, ('head', 'sec'), [(d, d ^ mask) for d in range(ways)])]
    ppermute x0 -> x7, waiting for transfers between devices: none -> 6.45 us  [on_device(): lax.ppermute(part, ('head', 'sec'), [(d, d ^ mask) for d in range(ways)])]
    all_to_all x0 -> x1, starting transfers between devices: none -> 4.82 us  [on_device(): lax.all_to_all(copies, ('head', 'sec'), split_axis=1, concat_axis=1, tile...]
    dynamic_update_slice x0 -> x7, local copies, waits for them, and re-layouts: none -> 4.56 us  [on_device(): lax.dynamic_update_slice_in_dim(partial_back, part, (here ^ mask) * heigh...]
  transfers between devices with their start and end apart: 2 -> 10, of which waited for: 2 -> 5; matrix products, arithmetic and copies ran while one was open for 1% -> 3% of each run, Pallas kernels for 0% -> 0%
where the time goes in v1:
time: 188 us; the launch traced here: 187 us
  waiting for transfers between devices  77.3 us (41%)
  matrix products  34.2 us (18%)
  local copies, waits for them, and re-layouts  32.1 us (17%)
  between operations  14.3 us (8%)
  starting transfers between devices  13.1 us (7%)
  blocking collectives  8.28 us (4%)
  other arithmetic  7.98 us (4%)
    reduce_scatter x1, waiting for transfers between devices, on_device(): lax.psum_scatter(partial_value.astype(jnp.bfloat16).astype(jnp.float32).a...  32.8 us
    all_to_all x1, waiting for transfers between devices, on_device(): lax.all_to_all(copies, ('head', 'sec'), split_axis=1, concat_axis=1, tile...  20.1 us
    reduce_scatter x1, waiting for transfers between devices, on_device(): lax.psum_scatter(partial_back.astype(jnp.float32).astype(jnp.bfloat16), '...  17.8 us
    dot_general x1, matrix products, run_expert(): jnp.dot(activated, down_weight[0], preferred_element_type=jnp.float32)  15.6 us
    all_gather x1, blocking collectives, on_device(): copies = lax.all_gather(buffer[None], 'req', axis=0, tiled=True)  8.28 us
    ppermute x7, starting transfers between devices, on_device(): lax.ppermute(part, ('head', 'sec'), [(d, d ^ mask) for d in range(ways)])  8.05 us
    dot_general x1, matrix products, run_expert(): jnp.dot(flat_rows, gate_weight[0], preferred_element_type=jnp.float32)  6.69 us
    gather x2, local copies, waits for them, and re-layouts, on_device(): sequence = cache_pool[block_table[0]]  6.47 us
  transfers between devices with their start and end apart: 10, of which 5 were waited for; matrix products, arithmetic and copies ran while one was open for 3% of the time, Pallas kernels for 0%

profile of v1, /device:TPU:0, one launch (start us, length us, event | category | flops | bytes accessed | tf_op | source)
XLA Modules:
  0.0 187.2 jit_solution(1635753682416524533)
XLA Ops:
  7.4 4.3 %gather_fusion = bf16[12,128,2,128]{3,2,1,0:T(2,128)(2,1)} fusion(bf16[12,128,2,128]{3,2,1,0:T(2,128)(2,1)} %param.13, s32[1024]{0:T(1024)S(1)} %pad_clamp_fusion.3), kind=kCustom, calls=%fused_computation | custom fusion | bytes 1572912 | tf_op jit(solution)/shard_map/gather | solution.py:55
  11.7 2.2 %copy.55 = bf16[12,128,2,128]{3,1,2,0:T(8,128)(2,1)} copy(bf16[12,128,2,128]{3,2,1,0:T(2,128)(2,1)} %gather_fusion) | data formatting | bytes 1572864 | tf_op jit(solution)/shard_map/gather | solution.py:55
  13.9 3.7 %gather_fusion.1 = bf16[8,12,128,128]{3,2,1,0:T(8,128)(2,1)} fusion(bf16[12,128,2,128]{3,1,2,0:T(8,128)(2,1)} %copy.55, s32[1024]{0:T(1024)S(1)} %pad_clamp_fusion.2), kind=kCustom, calls=%fused_computation.1 | custom fusion | bytes 6291488 | tf_op jit(solution)/shard_map/jit(_take)/gather | solution.py:59
  17.6 2.3 %select_bitcast_fusion = bf16[12,128,8,128]{3,1,0,2:T(8,128)(2,1)S(1)} fusion(bf16[8,12,128,128]{3,2,1,0:T(8,128)(2,1)} %gather_fusion.1, pred[8]{0:T(512)(128)(4,1)S(1)} %compare_and_fusion), kind=kLoop, calls=%fused_computation.18 | loop fusion | flops 1572864 | bytes 6291464 | tf_op jit(solution)/shard_map/jit(_take)/select_n | solution.py:59
  19.9 3.8 %fusion.50 = (bf16[12,128,8,64]{3,1,0,2:T(8,128)(2,1)}, bf16[12,128,8,64]{3,1,0,2:T(8,128)(2,1)}) fusion(bf16[12,128,8,128]{3,1,0,2:T(8,128)(2,1)S(1)} %select_bitcast_fusion), kind=kLoop, calls=%fused_computation.96 | loop fusion | bytes 6291456 | tf_op jit(solution)/shard_map/slice | solution.py:60
  24.7 4.1 %fusion.51 = f32[8,128]{1,0:T(8,128)S(1)} fusion(pred[128,1536]{0,1:T(8,128)(4,1)S(1)} %iota_compare_fusion, bf16[1536,8,64]{2,0,1:T(8,128)(2,1)} %bitcast.67, bf16[128,8,64]{0,2,1:T(8,128)(2,1)S(1)} %bitcast.72), kind=kOutput, calls=%fused_computation.97 | convolution fusion | flops 207619584 | bytes 1904640 | tf_op jit(solution)/shard_map/sub | solution.py:68
  28.7 5.8 %fusion.24 = bf16[8,64,128]{2,1,0:T(8,128)(2,1)S(1)} fusion(bf16[1536,8,64]{2,0,1:T(8,128)(2,1)} %bitcast.69, f32[8,128]{1,0:T(8,128)S(1)} %fusion.51, pred[128,1536]{0,1:T(8,128)(4,1)S(1)} %iota_compare_fusion, bf16[1536,8,64]{2,0,1:T(8,128)(2,1)} %bitcast.68, bf16[128,8,64]{0,2,1:T(8,128)(2,1)S(1)} %bitcast.73), kind=kOutput, calls=%fused_computation.26 | convolution fusion | flops 410585600 | bytes 3608576 | tf_op jit(solution)/shard_map/hnt,thd->nhd/dot_general | solution.py:71
  34.6 2.0 %convolution_convert_fusion = bf16[128,2880]{1,0:T(8,128)(2,1)} fusion(bf16[128,512]{0,1:T(8,128)(2,1)S(1)} %bitcast.74, bf16[512,2880]{0,1:T(8,128)(2,1)S(1)} %copy-done), kind=kOutput, calls=%fused_computation.17 | convolution fusion | flops 377856000 | bytes 3817472 | tf_op jit(solution)/shard_map/dot_general | solution.py:76
  38.2 32.8 %reduce-scatter.3.cloned.1.call-done = bf16[16,2880]{1,0:T(8,128)(2,1)} async-done(((bf16[128,2880]{1,0:T(8,128)(2,1)}), bf16[16,2880]{1,0:T(8,128)(2,1)}) %reduce-scatter.3.cloned.1.call-update) | async-done | bytes 92176 | tf_op jit(solution)/shard_map/reduce_scatter | solution.py:77
  73.8 8.3 %all_gather.3 = bf16[2,8,8,2880]{3,2,1,0:T(8,128)(2,1)S(1)} all-gather(bf16[1,8,8,2880]{3,2,1,0:T(8,128)(2,1)S(1)} %bitcast.71), channel_id=1, replica_groups=mesh['groups'=2,'req'=2,'head'=4,'sec'=2] {'req'}, dimensions={0}, use_global_device_ids=true | all-gather | bytes 1105920 | tf_op jit(solution)/shard_map/all_gather | solution.py:101
  83.0 4.8 %all-to-all-start = ((bf16[2,8,8,2880]{3,2,0,1:T(8,128)(2,1)}), bf16[2,8,8,2880]{3,2,0,1:T(8,128)(2,1)}, u32[]{:S(2)}, u32[]{:S(2)}) async-start(bf16[2,8,8,2880]{3,2,0,1:T(8,128)(2,1)} %copy.63), calls=%async_computation.1 | async-start | bytes 1507328 | tf_op jit(solution)/shard_map/all_to_all | solution.py:103
  88.1 20.1 %all-to-all-done = bf16[2,8,8,2880]{3,2,0,1:T(8,128)(2,1)} async-done(((bf16[2,8,8,2880]{3,2,0,1:T(8,128)(2,1)}), bf16[2,8,8,2880]{3,2,0,1:T(8,128)(2,1)}, u32[]{:S(2)}, u32[]{:S(2)}) %all-to-all-start) | async-done | bytes 737312 | tf_op jit(solution)/shard_map/all_to_all | solution.py:103
  110.3 6.7 %fusion.5 = f32[128,1440]{0,1:T(8,128)} fusion(bf16[128,2880]{1,0:T(8,128)(2,1)S(1)} %bitcast.65, bf16[1,2880,1440]{1,2,0:T(8,128)(2,1)} %param.21), kind=kOutput, calls=%fused_computation.10 | convolution fusion | flops 1061683200 | bytes 9768960 | tf_op jit(solution)/shard_map/dot_general | solution.py:17
  117.0 15.6 %fusion.8 = bf16[128,2880]{0,1:T(8,128)(2,1)} fusion(bf16[1,1440,2880]{2,1,0:T(8,128)(2,1)} %param.23, bf16[128,2880]{1,0:T(8,128)(2,1)} %bitcast.66, bf16[1,2880,1440]{1,2,0:T(8,128)(2,1)} %param.22, f32[128,1440]{0,1:T(8,128)} %fusion.5), kind=kOutput, calls=%fused_computation.16 | convolution fusion | flops 2125209600 | bytes 18800640 | tf_op jit(solution)/shard_map/dot_general | solution.py:20
  132.6 2.3 %copy.65 = bf16[128,2880]{1,0:T(8,128)(2,1)} copy(bf16[128,2880]{0,1:T(8,128)(2,1)} %fusion.8) | data formatting | bytes 1474560 | tf_op jit(solution)/shard_map/convert_element_type | solution.py:21
  135.8 1.9 %constant_dynamic-slice_fusion.6 = (bf16[2,1,8,2880]{3,2,1,0:T(8,128)(2,1)S(1)}, bf16[2,1,8,2880]{3,2,1,0:T(8,128)(2,1)S(1)}, bf16[2,1,8,2880]{3,2,1,0:T(8,128)(...) fusion(bf16[2,8,8,2880]{3,2,1,0:T(8,128)(2,1)} %bitcast.70, ...), kind=kLoop, calls=%fused_computation.61 | loop fusion | bytes 1493024 | tf_op jit(solution)/shard_map/dynamic_slice | solution.py:116
  137.7 1.9 collective-permute-start.2
  139.7 2.4 %collective-permute-start.4 = (bf16[2,1,8,2880]{3,2,1,0:T(8,128)(2,1)S(1)}, bf16[2,1,8,2880]{3,2,1,0:T(8,128)(2,1)S(1)}, u32[]{:S(2)}, u32[]{:S(2)}) collective-permute-start(bf16[2,1,8,2880]{3,2,1,0:T(8,128)(2,1)S(1)} %get-tuple-element.9), channel_id=1, source_target_pairs={{0,5},{1,4},{2,7},{3,6},{4,1},{5,0},{6,3},{7,2},{8,13},{9,12},{10,... | collective-permute-start | bytes 276488 | tf_op jit(solution)/shard_map/ppermute | solution.py:118
  142.1 1.3 collective-permute-start.5
  144.1 2.3 %collective-permute-start.6 = (bf16[2,1,8,2880]{3,2,1,0:T(8,128)(2,1)S(1)}, bf16[2,1,8,2880]{3,2,1,0:T(8,128)(2,1)S(1)}, u32[]{:S(2)}, u32[]{:S(2)}) collective-permute-start(bf16[2,1,8,2880]{3,2,1,0:T(8,128)(2,1)S(1)} %get-tuple-element.7), channel_id=1, source_target_pairs={{0,7},{1,6},{2,5},{3,4},{4,3},{5,2},{6,1},{7,0},{8,15},{9,14},{10,... | collective-permute-start | bytes 276488 | tf_op jit(solution)/shard_map/ppermute | solution.py:118
  147.7 6.4 %collective-permute-done.3 = bf16[2,1,8,2880]{3,2,1,0:T(8,128)(2,1)S(1)} collective-permute-done((bf16[2,1,8,2880]{3,2,1,0:T(8,128)(2,1)S(1)}, bf16[2,1,8,2880]{3,2,1,0:T(8,128)(2,1)S(1)}, u32[]{:S(2)}, u32[]{:S(2)}) %collective-permute-start.3) | collective-permute-done | bytes 92192 | tf_op jit(solution)/shard_map/ppermute | solution.py:118
  156.9 17.8 %reduce-scatter.5.cloned.1.call-done = bf16[1,8,8,2880]{3,2,1,0:T(8,128)(2,1)} async-done(((bf16[2,8,8,2880]{3,2,1,0:T(8,128)(2,1)}), bf16[1,8,8,2880]{3,2,1,0:T(8,128)(2,1)}) %reduce-scatter.5.cloned.1.call-update) | async-done | bytes 368656 | tf_op jit(solution)/shard_map/reduce_scatter | solution.py:123
  174.7 2.2 %gather_fusion.3 = bf16[64,2880]{1,0:T(8,128)(2,1)S(1)} fusion(bf16[64,2880]{1,0:T(8,128)(2,1)} %bitcast.64, s32[1024]{0:T(1024)S(1)} %pad_clamp_fusion), kind=kCustom, calls=%fused_computation.3 | custom fusion | bytes 737536 | tf_op jit(solution)/shard_map/gather | solution.py:132
  178.0 1.7 multiply_reduce_fusion
  (68 shorter events, 16.2 us)
Async XLA Ops:
  6.5 28.1 %copy-start = (bf16[512,2880]{0,1:T(8,128)(2,1)S(1)}, bf16[512,2880]{0,1:T(8,128)(2,1)}, u32[]{:S(2)}) copy-start(bf16[512,2880]{0,1:T(8,128)(2,1)} %param.16) | copy-start | bytes 8847364
  6.5 64.5 %reduce-scatter.3.cloned.1.call-start = ((), (), s32[]{:S(2)}) async-start(), calls=%async_computation.3 | async-start | bytes 847872 | tf_op jit(solution)/shard_map/reduce_scatter | solution.py:77
  19.9 4.7 %copy-start.4 = (bf16[128,512]{1,0:T(8,128)(2,1)S(1)}, bf16[128,512]{1,0:T(8,128)(2,1)}, u32[]{:S(2)}) copy-start(bf16[128,512]{1,0:T(8,128)(2,1)} %param.12) | copy-start | bytes 393220
  34.6 2.1 %copy-start.6 = (s32[16,4]{0,1:T(4,128)S(1)}, s32[16,4]{0,1:T(4,128)}, u32[]{:S(2)}) copy-start(s32[16,4]{0,1:T(4,128)} %param.19) | copy-start | bytes 772
  34.6 36.4 %copy-start.2 = (bf16[16,2880]{1,0:T(8,128)(2,1)S(1)}, bf16[16,2880]{1,0:T(8,128)(2,1)}, u32[]{:S(2)}) copy-start(bf16[16,2880]{1,0:T(8,128)(2,1)} %param.17) | copy-start | bytes 276484
  34.6 37.5 %copy-start.5 = (f32[2880]{0:T(1024)S(1)}, f32[2880]{0:T(1024)}, u32[]{:S(2)}) copy-start(f32[2880]{0:T(1024)} %param.18) | copy-start | bytes 34564
  83.0 25.2 %all-to-all-start = ((bf16[2,8,8,2880]{3,2,0,1:T(8,128)(2,1)}), bf16[2,8,8,2880]{3,2,0,1:T(8,128)(2,1)}, u32[]{:S(2)}, u32[]{:S(2)}) async-start(bf16[2,8,8,2880]{3,2,0,1:T(8,128)(2,1)} %copy.63), calls=%async_computation.1 | async-start | bytes 1507328 | tf_op jit(solution)/shard_map/all_to_all | solution.py:103
  87.9 86.9 %reduce-scatter.5.cloned.1.call-start = ((), (), s32[]{:S(2)}) async-start(), calls=%async_computation.4 | async-start | bytes 1130496 | tf_op jit(solution)/shard_map/reduce_scatter | solution.py:123
  109.4 0.9 copy-start.1
  132.6 24.2 %copy-start.7 = (f32[16,4]{0,1:T(4,128)S(1)}, f32[16,4]{0,1:T(4,128)}, u32[]{:S(2)}) copy-start(f32[16,4]{0,1:T(4,128)} %param.20) | copy-start | bytes 772
  137.7 4.4 %collective-permute-start = (bf16[2,1,8,2880]{3,2,1,0:T(8,128)(2,1)S(1)}, bf16[2,1,8,2880]{3,2,1,0:T(8,128)(2,1)S(1)}, u32[]{:S(2)}, u32[]{:S(2)}) collective-permute-start(bf16[2,1,8,2880]{3,2,1,0:T(8,128)(2,1)S(1)} %get-tuple-element.13), channel_id=1, source_target_pairs={{0,1},{1,0},{2,3},{3,2},{4,5},{5,4},{6,7},{7,6},{8,9},{9,8},{10,11... | collective-permute-start | bytes 276488 | tf_op jit(solution)/shard_map/ppermute | solution.py:118
  137.7 6.4 %collective-permute-start.1 = (bf16[2,1,8,2880]{3,2,1,0:T(8,128)(2,1)S(1)}, bf16[2,1,8,2880]{3,2,1,0:T(8,128)(2,1)S(1)}, u32[]{:S(2)}, u32[]{:S(2)}) collective-permute-start(bf16[2,1,8,2880]{3,2,1,0:T(8,128)(2,1)S(1)} %get-tuple-element.12), channel_id=1, source_target_pairs={{0,2},{1,3},{2,0},{3,1},{4,6},{5,7},{6,4},{7,5},{8,10},{9,11},{10,... | collective-permute-start | bytes 276488 | tf_op jit(solution)/shard_map/ppermute | solution.py:118
  137.7 9.3 %collective-permute-start.2 = (bf16[2,1,8,2880]{3,2,1,0:T(8,128)(2,1)S(1)}, bf16[2,1,8,2880]{3,2,1,0:T(8,128)(2,1)S(1)}, u32[]{:S(2)}, u32[]{:S(2)}) collective-permute-start(bf16[2,1,8,2880]{3,2,1,0:T(8,128)(2,1)S(1)} %get-tuple-element.11), channel_id=1, source_target_pairs={{0,3},{1,2},{2,1},{3,0},{4,7},{5,6},{6,5},{7,4},{8,11},{9,10},{10,... | collective-permute-start | bytes 276488 | tf_op jit(solution)/shard_map/ppermute | solution.py:118
  139.6 14.5 %collective-permute-start.3 = (bf16[2,1,8,2880]{3,2,1,0:T(8,128)(2,1)S(1)}, bf16[2,1,8,2880]{3,2,1,0:T(8,128)(2,1)S(1)}, u32[]{:S(2)}, u32[]{:S(2)}) collective-permute-start(bf16[2,1,8,2880]{3,2,1,0:T(8,128)(2,1)S(1)} %get-tuple-element.10), channel_id=1, source_target_pairs={{0,4},{1,5},{2,6},{3,7},{4,0},{5,1},{6,2},{7,3},{8,12},{9,13},{10,... | collective-permute-start | bytes 276488 | tf_op jit(solution)/shard_map/ppermute | solution.py:118
  139.7 15.1 %collective-permute-start.4 = (bf16[2,1,8,2880]{3,2,1,0:T(8,128)(2,1)S(1)}, bf16[2,1,8,2880]{3,2,1,0:T(8,128)(2,1)S(1)}, u32[]{:S(2)}, u32[]{:S(2)}) collective-permute-start(bf16[2,1,8,2880]{3,2,1,0:T(8,128)(2,1)S(1)} %get-tuple-element.9), channel_id=1, source_target_pairs={{0,5},{1,4},{2,7},{3,6},{4,1},{5,0},{6,3},{7,2},{8,13},{9,12},{10,... | collective-permute-start | bytes 276488 | tf_op jit(solution)/shard_map/ppermute | solution.py:118
  142.1 13.4 %collective-permute-start.5 = (bf16[2,1,8,2880]{3,2,1,0:T(8,128)(2,1)S(1)}, bf16[2,1,8,2880]{3,2,1,0:T(8,128)(2,1)S(1)}, u32[]{:S(2)}, u32[]{:S(2)}) collective-permute-start(bf16[2,1,8,2880]{3,2,1,0:T(8,128)(2,1)S(1)} %get-tuple-element.8), channel_id=1, source_target_pairs={{0,6},{1,7},{2,4},{3,5},{4,2},{5,3},{6,0},{7,1},{8,14},{9,15},{10,... | collective-permute-start | bytes 276488 | tf_op jit(solution)/shard_map/ppermute | solution.py:118
  144.1 12.0 %collective-permute-start.6 = (bf16[2,1,8,2880]{3,2,1,0:T(8,128)(2,1)S(1)}, bf16[2,1,8,2880]{3,2,1,0:T(8,128)(2,1)S(1)}, u32[]{:S(2)}, u32[]{:S(2)}) collective-permute-start(bf16[2,1,8,2880]{3,2,1,0:T(8,128)(2,1)S(1)} %get-tuple-element.7), channel_id=1, source_target_pairs={{0,7},{1,6},{2,5},{3,4},{4,3},{5,2},{6,1},{7,0},{8,15},{9,14},{10,... | collective-permute-start | bytes 276488 | tf_op jit(solution)/shard_map/ppermute | solution.py:118
  156.8 22.9 %copy-start.3 = (bf16[16,2880]{1,0:T(8,128)(2,1)S(1)}, bf16[16,2880]{1,0:T(8,128)(2,1)}, u32[]{:S(2)}) copy-start(bf16[16,2880]{1,0:T(8,128)(2,1)} %reduce-scatter.3.cloned.1.call-done) | copy-start | bytes 276484
Sparse Core Ops, SparseCore 0:
  36.7 34.2 reduce-scatter.2
  156.9 17.7 reduce-scatter.4
